TPU v7x, 512 devices: a whole 4x8x8 slice. The times are simulated.
512 devices in a mesh: dp: 32 (over z, x), param: 16 (over y, core).
Axes of the slice: x: 4, y: 8, z: 8, core: 2. Of those that a mesh axis runs over, the one named last changes fastest.
Arguments:
- features: bfloat16 [32768, 2048], P('dp'), may hold values from -24 to 24
- w_hidden: bfloat16 [2048, 2048], P(None, 'param'), may hold values from -0.125 to 0.125
- w_head: bfloat16 [2048, 36], P('param'), may hold values from -0.03125 to 0.03125
- base_mean: float32 [32768, 36], P('dp'), may hold values from -5 to 5
- actions: float32 [32768, 36], P('dp'), may hold values from -7 to 7
- advantages: float32 [32768], P('dp'), may hold values from -4 to 4
- log_std: float32 [36], replicated, may hold values from -1 to 0
Outputs:
- step_unit: float32 [2048, 2048], P('dp', 'param')
- kl_ratio: float32 [], replicated
All inputs are finite; a program needn't handle non-finite values.
Results may differ from a plain program's by a relative error of at most 0.0049.
Values may be sent and summed in bfloat16 or wider, within the bound.
A program may use at most 64 MiB of HBM per device.

v0:
```python
import jax
import jax.numpy as jnp
from jax import lax
from jax.sharding import PartitionSpec as P

D = 2048
UNITS = 2048
ITERS = 2
DAMPING = 0.01
TRIAL_KL = 4.0


def shards(features, w_hidden, w_head, base_mean, actions, advantages, log_std):
    highest = lax.Precision.HIGHEST
    rows = features.shape[0]
    width = features.shape[1]
    dp_count = lax.axis_size("dp")
    batch = rows * dp_count
    inv_var = jnp.exp(-2.0 * log_std)
    pre = jnp.dot(features, w_hidden, preferred_element_type=jnp.float32)
    hidden = jnp.tanh(pre)
    slope = 1.0 - hidden * hidden

    def head_total(part):
        return lax.psum(jnp.dot(part, w_head, preferred_element_type=jnp.float32), "param")

    mean = base_mean + head_total(hidden.astype(jnp.bfloat16))
    delta = advantages[:, None] * (actions - mean) * inv_var
    head_t = w_head.astype(jnp.float32).T

    def pull(moment):
        return (jnp.dot(moment, head_t, precision=highest) * slope / batch).astype(jnp.bfloat16)

    def rowsum(grads):
        term = lax.dot_general(
            features, grads, (((0,), (0,)), ((), ())), preferred_element_type=jnp.float32
        )
        return lax.psum(term, "dp")

    def expand(vector_b):
        return jnp.dot(features, vector_b, preferred_element_type=jnp.float32)

    def total(values):
        return lax.psum((values[0],), "param")

    grad = rowsum(pull(delta))
    solution = jnp.zeros_like(grad)
    resid = grad
    direction = grad
    (norm_now,) = total((jnp.sum(resid * resid),))
    for turn in range(ITERS):
        change = expand(direction.astype(jnp.bfloat16))
        dmu = head_total((change * slope).astype(jnp.bfloat16))
        image = rowsum(pull(dmu * inv_var)) + DAMPING * direction
        image, dmu = (image, dmu)
        (curv,) = total((jnp.sum(direction * image),))
        alpha = norm_now / curv
        solution = solution + alpha * direction
        resid = resid - alpha * image
        (norm_next,) = total((jnp.sum(resid * resid),))
        direction = resid + norm_next / norm_now * direction
        norm_now = norm_next
    (shs,) = total((jnp.sum(solution * (grad - resid)),))
    block = width // dp_count
    step_unit = lax.dynamic_slice_in_dim(
        solution * jnp.sqrt(D * UNITS / shs), lax.axis_index("dp") * block, block, 0
    )
    reach = jnp.sqrt(2.0 * TRIAL_KL / shs)
    moved = expand((reach * solution).astype(jnp.bfloat16))
    shift = (jnp.tanh(pre + moved) - hidden).astype(jnp.bfloat16)
    dmean = head_total(shift)
    kl_value = lax.psum(jnp.sum(dmean * dmean * inv_var) / (2.0 * batch), "dp")
    return (step_unit, kl_value / TRIAL_KL)


def solution(mesh):
    return jax.shard_map(
        shards,
        mesh=mesh,
        in_specs=(
            P("dp", None),
            P(None, "param"),
            P("param", None),
            P("dp", None),
            P("dp", None),
            P("dp"),
            P(),
        ),
        out_specs=(P("dp", "param"), P()),
        check_vma=False,
    )
```

profile of v0, /device:TPU:8, one launch (start us, length us, event | category | flops | bytes accessed | tf_op | source)
XLA Modules:
  0.0 1150.3 jit_solution(4026722061031804049)
XLA Ops:
  7.2 0.0 copy-start
  7.2 0.0 copy-start.3
  7.2 0.0 all-reduce.9.cloned.1.call-start
  7.3 0.9 copy-done
  8.2 3.4 fusion.42
  11.7 0.9 fusion.27
  12.6 0.0 all-reduce.9.cloned.1.call-update
  12.6 0.0 all-reduce.11.cloned.1.call-start
  12.7 112.3 %all-reduce.9.cloned.1.call-done = f32[1024,36]{0,1:T(8,128)} async-done(((f32[1024,36]{0,1:T(8,128)}), f32[1024,36]{0,1:T(8,128)}) %all-reduce.9.cloned.1.call-update) | async-done | bytes 147472 | tf_op jit(solution)/shard_map/psum | solution.py:25
  125.0 0.0 copy-done.4
  125.0 1.6 fusion.11
  126.6 4.0 convolution_bitcast_fusion.2
  130.5 0.0 all-reduce.11.cloned.1.call-update
  130.6 0.0 all-reduce.13.cloned.1.call-start
  130.6 160.6 %all-reduce.11.cloned.1.call-done = f32[2048,128]{0,1:T(8,128)} async-done(((f32[2048,128]{0,1:T(8,128)}), f32[2048,128]{0,1:T(8,128)}) %all-reduce.11.cloned.1.call-update) | async-done | bytes 1048592 | tf_op jit(solution)/shard_map/psum | solution.py:38
  291.2 4.7 fusion.16
  295.9 0.0 all-reduce.13.cloned.1.call-update
  295.9 0.0 all-reduce.15.cloned.1.call-start
  296.0 104.9 %all-reduce.13.cloned.1.call-done = f32[1024,36]{0,1:T(8,128)} async-done(((f32[1024,36]{0,1:T(8,128)}), f32[1024,36]{0,1:T(8,128)}) %all-reduce.13.cloned.1.call-update) | async-done | bytes 147472 | tf_op jit(solution)/shard_map/psum | solution.py:25
  400.8 1.6 fusion.10
  402.4 3.9 convolution_bitcast_fusion.1
  406.4 0.0 all-reduce.15.cloned.1.call-update
  406.4 0.0 all-reduce.17.cloned.1.call-start
  406.4 160.6 %all-reduce.15.cloned.1.call-done = f32[2048,128]{0,1:T(8,128)} async-done(((f32[2048,128]{0,1:T(8,128)}), f32[2048,128]{0,1:T(8,128)}) %all-reduce.15.cloned.1.call-update) | async-done | bytes 1048592 | tf_op jit(solution)/shard_map/psum | solution.py:38
  567.0 2.2 multiply_reduce_fusion.3
  569.2 21.2 %all-reduce = (f32[]{:T(128)}, f32[]{:T(128)}) all-reduce(f32[]{:T(128)} %get-tuple-element.5, f32[]{:T(128)} %get-tuple-element.4), channel_id=1, replica_groups=mesh['dp'=32,'param'=16] {'param'}, use_global_device_ids=true, to_apply=%region_3.0 | all-reduce | flops 2 | bytes 16 | tf_op jit(solution)/shard_map/psum | solution.py:44
  591.8 2.1 multiply_reduce_fusion.2
  593.9 24.2 %psum.97 = f32[]{:T(128)} all-reduce(f32[]{:T(128)} %multiply_reduce_fusion.2), channel_id=1, replica_groups=mesh['dp'=32,'param'=16] {'param'}, use_global_device_ids=true, to_apply=%region_9.0 | all-reduce | flops 1 | bytes 8 | tf_op jit(solution)/shard_map/psum | solution.py:44
  619.4 4.4 fusion.15
  623.7 0.0 all-reduce.17.cloned.1.call-update
  623.8 0.0 all-reduce.19.cloned.1.call-start
  623.8 107.6 %all-reduce.17.cloned.1.call-done = f32[1024,36]{0,1:T(8,128)} async-done(((f32[1024,36]{0,1:T(8,128)}), f32[1024,36]{0,1:T(8,128)}) %all-reduce.17.cloned.1.call-update) | async-done | bytes 147472 | tf_op jit(solution)/shard_map/psum | solution.py:25
  731.4 1.6 fusion.9
  733.0 3.9 convolution_bitcast_fusion
  737.0 0.0 all-reduce.19.cloned.1.call-update
  737.0 0.0 all-reduce.21.cloned.1.call-start
  737.0 160.6 %all-reduce.19.cloned.1.call-done = f32[2048,128]{0,1:T(8,128)} async-done(((f32[2048,128]{0,1:T(8,128)}), f32[2048,128]{0,1:T(8,128)}) %all-reduce.19.cloned.1.call-update) | async-done | bytes 1048592 | tf_op jit(solution)/shard_map/psum | solution.py:38
  897.6 2.2 multiply_reduce_fusion.1
  899.8 21.2 %psum.100 = f32[]{:T(128)} all-reduce(f32[]{:T(128)} %multiply_reduce_fusion.1), channel_id=1, replica_groups=mesh['dp'=32,'param'=16] {'param'}, use_global_device_ids=true, to_apply=%region_13.0 | all-reduce | flops 1 | bytes 8 | tf_op jit(solution)/shard_map/psum | solution.py:44
  922.4 3.4 multiply_reduce_fusion
  925.7 24.2 %psum.101 = f32[]{:T(128)} all-reduce(f32[]{:T(128)} %get-tuple-element.8), channel_id=1, replica_groups=mesh['dp'=32,'param'=16] {'param'}, use_global_device_ids=true, to_apply=%region_15.0 | all-reduce | flops 1 | bytes 8 | tf_op jit(solution)/shard_map/psum | solution.py:44
  950.6 4.6 fusion.14
  955.2 0.0 all-reduce.21.cloned.1.call-update
  955.9 0.9 dynamic-slice_multiply_fusion
  956.8 106.1 %all-reduce.21.cloned.1.call-done = f32[1024,36]{0,1:T(8,128)} async-done(((f32[1024,36]{0,1:T(8,128)}), f32[1024,36]{0,1:T(8,128)}) %all-reduce.21.cloned.1.call-update) | async-done | bytes 147472 | tf_op jit(solution)/shard_map/psum | solution.py:25
  1062.9 1.6 multiply_reduce_fusion.5
  1065.2 0.7 copy.9
  1065.9 75.8 %psum.103 = f32[]{:T(128)} all-reduce(f32[]{:T(128)S(6)} %div.38), channel_id=1, replica_groups=mesh['dp'=32,'param'=16] {'dp'}, use_global_device_ids=true, to_apply=%region_18.0 | all-reduce | flops 1 | bytes 8 | tf_op jit(solution)/shard_map/psum | solution.py:72
  (13 shorter events, 0.0 us)
Async XLA Ops:
  7.2 1.0 copy-start
  7.2 4.5 copy-start.3
  7.2 5.5 copy-start.7
  7.2 117.8 %copy-start.5 = (f32[1024,36]{0,1:T(8,128)S(1)}, f32[1024,36]{0,1:T(8,128)}, u32[]{:S(2)}) copy-start(f32[1024,36]{0,1:T(8,128)} %param.10) | copy-start | bytes 442372
  7.2 117.8 %copy-start.4 = (f32[1024,36]{0,1:T(8,128)S(1)}, f32[1024,36]{0,1:T(8,128)}, u32[]{:S(2)}) copy-start(f32[1024,36]{0,1:T(8,128)} %param.11) | copy-start | bytes 442372
  7.2 117.8 %copy-start.6 = (f32[1024]{0:T(1024)S(1)}, f32[1024]{0:T(1024)}, u32[]{:S(2)}) copy-start(f32[1024]{0:T(1024)} %param.12) | copy-start | bytes 12292
  7.2 117.7 %all-reduce.9.cloned.1.call-start = ((), (), s32[]{:S(2)}) async-start(), calls=%async_computation | async-start | bytes 327680 | tf_op jit(solution)/shard_map/psum | solution.py:25
  12.6 278.6 %all-reduce.11.cloned.1.call-start = ((), (), s32[]{:S(2)}) async-start(), calls=%async_computation.1 | async-start | bytes 2097152 | tf_op jit(solution)/shard_map/psum | solution.py:38
  130.6 270.3 %all-reduce.13.cloned.1.call-start = ((), (), s32[]{:S(2)}) async-start(), calls=%async_computation.2 | async-start | bytes 327680 | tf_op jit(solution)/shard_map/psum | solution.py:25
  295.9 271.1 %copy-start.1 = (f32[2048,128]{0,1:T(8,128)S(1)}, f32[2048,128]{0,1:T(8,128)}, u32[]{:S(2)}) copy-start(f32[2048,128]{0,1:T(8,128)} %all-reduce.11.cloned.1.call-done) | copy-start | bytes 3145732
  295.9 271.1 %all-reduce.15.cloned.1.call-start = ((), (), s32[]{:S(2)}) async-start(), calls=%async_computation.3 | async-start | bytes 2097152 | tf_op jit(solution)/shard_map/psum | solution.py:38
  406.4 325.1 %all-reduce.17.cloned.1.call-start = ((), (), s32[]{:S(2)}) async-start(), calls=%async_computation.4 | async-start | bytes 327680 | tf_op jit(solution)/shard_map/psum | solution.py:25
  567.0 52.4 %copy-start.2 = (f32[2048,128]{0,1:T(8,128)S(1)}, f32[2048,128]{0,1:T(8,128)}, u32[]{:S(2)}) copy-start(f32[2048,128]{0,1:T(8,128)} %all-reduce.15.cloned.1.call-done) | copy-start | bytes 3145732
  623.8 273.8 %all-reduce.19.cloned.1.call-start = ((), (), s32[]{:S(2)}) async-start(), calls=%async_computation.5 | async-start | bytes 2097152 | tf_op jit(solution)/shard_map/psum | solution.py:38
  737.0 325.9 %all-reduce.21.cloned.1.call-start = ((), (), s32[]{:S(2)}) async-start(), calls=%async_computation.6 | async-start | bytes 327680 | tf_op jit(solution)/shard_map/psum | solution.py:25
Sparse Core Ops, SparseCore 0:
  12.7 112.1 all-reduce.8
  130.7 160.5 all-reduce.10
  296.1 104.7 all-reduce.12
  406.5 160.4 all-reduce.14
  623.9 107.4 all-reduce.16
  737.1 160.4 all-reduce.18
  955.3 107.5 all-reduce.20
where the time goes:
time: 1150 us
  waiting for transfers between devices  913 us (79%)
  blocking collectives  167 us (15%)
  matrix products  34.5 us (3%)
  between operations  22.2 us (2%)
  other arithmetic  12.4 us (1%)
    psum x3, waiting for transfers between devices, rowsum(): return lax.psum(term, 'dp')  482 us
    psum x4, waiting for transfers between devices, head_total(): lax.psum(jnp.dot(part, w_head, preferred_element_type=jnp.float32), 'param')  431 us
    psum x4, blocking collectives, total(): return lax.psum((values[0],), 'param')  90.8 us
    psum x1, blocking collectives, shards(): kl_value = lax.psum(jnp.sum(dmean * dmean * inv_var) / (2.0 * batch), 'dp')  75.8 us
  transfers between devices with their start and end apart: 7, of which 7 were waited for; matrix products, arithmetic and copies ran while one was open for 0% of the time, Pallas kernels for 0%

commit v1 on v0

--- a/solution.py
+++ b/solution.py
@@ -32,10 +32,15 @@
         return (jnp.dot(moment, head_t, precision=highest) * slope / batch).astype(jnp.bfloat16)
 
     def rowsum(grads):
+
+        def _detail_numbers(arr):
+            t_next = jnp.sum(lax.all_gather(arr, "dp"), axis=0)
+            return t_next
+
         term = lax.dot_general(
             features, grads, (((0,), (0,)), ((), ())), preferred_element_type=jnp.float32
         )
-        return lax.psum(term, "dp")
+        return _detail_numbers(term)
 
     def expand(vector_b):
         return jnp.dot(features, vector_b, preferred_element_type=jnp.float32)

time: 1150 us -> 1490 us (1.30)
  waiting for transfers between devices: 913 us -> 1140 us
  local copies, waits for them, and re-layouts: 1.67 us -> 87.3 us
  other arithmetic: 12.4 us -> 29.2 us
    all_gather x0 -> x3, waiting for transfers between devices: none -> 717 us  [_detail_numbers(): t_next = jnp.sum(lax.all_gather(arr, 'dp'), axis=0)]
    psum x3 -> x0, waiting for transfers between devices: 482 us -> none  [rowsum(): return lax.psum(term, 'dp')]
    unnamed x17 -> x20, local copies, waits for them, and re-layouts: 1.67 us -> 87.3 us
    reduce_sum x0 -> x3, other arithmetic: none -> 20.5 us  [_detail_numbers(): t_next = jnp.sum(lax.all_gather(arr, 'dp'), axis=0)]
where the time goes in v1:
time: 1490 us
  waiting for transfers between devices  1140 us (77%)
  blocking collectives  170 us (11%)
  local copies, waits for them, and re-layouts  87.3 us (6%)
  matrix products  34.2 us (2%)
  other arithmetic  29.2 us (2%)
  between operations  22.2 us (1%)
    all_gather x3, waiting for transfers between devices, _detail_numbers(): t_next = jnp.sum(lax.all_gather(arr, 'dp'), axis=0)  717 us
    psum x4, waiting for transfers between devices, head_total(): lax.psum(jnp.dot(part, w_head, preferred_element_type=jnp.float32), 'param')  425 us
    psum x4, blocking collectives, total(): return lax.psum((values[0],), 'param')  94.6 us
    unnamed x20, local copies, waits for them, and re-layouts  87.3 us
    psum x1, blocking collectives, shards(): kl_value = lax.psum(jnp.sum(dmean * dmean * inv_var) / (2.0 * batch), 'dp')  75.8 us
  transfers between devices with their start and end apart: 7, of which 7 were waited for; matrix products, arithmetic and copies ran while one was open for 0% of the time, Pallas kernels for 0%

profile of v1, /device:TPU:8, one launch (start us, length us, event | category | flops | bytes accessed | tf_op | source)
XLA Modules:
  0.0 1486.9 jit_solution(3468643227662195432)
XLA Ops:
  7.2 0.0 all-reduce.6.cloned.1.call-start
  7.3 0.9 copy-done
  8.2 3.4 fusion.42
  11.7 0.9 fusion.27
  12.6 0.0 all-reduce.6.cloned.1.call-update
  12.6 0.0 all-gather.7.cloned.1.call-start
  12.7 112.3 %all-reduce.6.cloned.1.call-done = f32[1024,36]{0,1:T(8,128)} async-done(((f32[1024,36]{0,1:T(8,128)}), f32[1024,36]{0,1:T(8,128)}) %all-reduce.6.cloned.1.call-update) | async-done | bytes 147472 | tf_op jit(solution)/shard_map/psum | solution.py:25
  125.0 1.6 fusion.11
  126.6 3.9 convolution_bitcast_fusion.2
  130.5 0.0 all-gather.7.cloned.1.call-update
  130.6 0.0 all-reduce.8.cloned.1.call-start
  130.6 239.3 %all-gather.7.cloned.1.call-done = f32[65536,128]{0,1:T(8,128)} async-done(((f32[2048,128]{0,1:T(8,128)}), f32[65536,128]{0,1:T(8,128)}) %all-gather.7.cloned.1.call-update) | async-done | bytes 33554448 | tf_op jit(solution)/shard_map/all_gather | solution.py:37
  369.9 28.2 %copy.10 = f32[16,8,32,2048]{3,2,1,0:T(8,128)S(1)} copy(f32[16,8,32,2048]{3,1,2,0:T(8,128)} %bitcast.68) | data formatting | bytes 67108864
  398.1 6.8 bitcast_reduce_fusion.2
  404.9 4.3 fusion.16
  409.2 0.0 all-gather.9.cloned.1.call-start
  409.3 104.2 %all-reduce.8.cloned.1.call-done = f32[1024,36]{0,1:T(8,128)} async-done(((f32[1024,36]{0,1:T(8,128)}), f32[1024,36]{0,1:T(8,128)}) %all-reduce.8.cloned.1.call-update) | async-done | bytes 147472 | tf_op jit(solution)/shard_map/psum | solution.py:25
  513.5 1.6 fusion.10
  515.1 3.9 convolution_bitcast_fusion.1
  519.0 0.0 all-gather.9.cloned.1.call-update
  519.0 0.2 all-reduce.10.cloned.1.call-start
  519.2 239.1 %all-gather.9.cloned.1.call-done = f32[65536,128]{0,1:T(8,128)} async-done(((f32[2048,128]{0,1:T(8,128)}), f32[65536,128]{0,1:T(8,128)}) %all-gather.9.cloned.1.call-update) | async-done | bytes 33554448 | tf_op jit(solution)/shard_map/all_gather | solution.py:37
  758.3 28.2 %copy.11 = f32[16,8,32,2048]{3,2,1,0:T(8,128)S(1)} copy(f32[16,8,32,2048]{3,1,2,0:T(8,128)} %bitcast.69) | data formatting | bytes 67108864
  786.5 6.8 bitcast_reduce_fusion.1
  793.3 0.9 multiply_reduce_fusion.3
  794.3 23.1 %all-reduce = (f32[]{:T(128)}, f32[]{:T(128)}) all-reduce(f32[]{:T(128)} %get-tuple-element.5, f32[]{:T(128)} %get-tuple-element.4), channel_id=1, replica_groups=mesh['dp'=32,'param'=16] {'param'}, use_global_device_ids=true, to_apply=%region_3.0 | all-reduce | flops 2 | bytes 16 | tf_op jit(solution)/shard_map/psum | solution.py:49
  818.7 0.9 multiply_reduce_fusion.2
  819.6 24.2 %psum.74 = f32[]{:T(128)} all-reduce(f32[]{:T(128)} %multiply_reduce_fusion.2), channel_id=1, replica_groups=mesh['dp'=32,'param'=16] {'param'}, use_global_device_ids=true, to_apply=%region_9.0 | all-reduce | flops 1 | bytes 8 | tf_op jit(solution)/shard_map/psum | solution.py:49
  845.1 4.4 fusion.15
  849.5 0.0 all-gather.11.cloned.1.call-start
  849.5 105.4 %all-reduce.10.cloned.1.call-done = f32[1024,36]{0,1:T(8,128)} async-done(((f32[1024,36]{0,1:T(8,128)}), f32[1024,36]{0,1:T(8,128)}) %all-reduce.10.cloned.1.call-update) | async-done | bytes 147472 | tf_op jit(solution)/shard_map/psum | solution.py:25
  954.9 1.6 fusion.9
  956.5 3.9 convolution_bitcast_fusion
  960.5 0.3 all-reduce.12.cloned.1.call-start
  960.7 239.0 %all-gather.11.cloned.1.call-done = f32[65536,128]{0,1:T(8,128)} async-done(((f32[2048,128]{0,1:T(8,128)}), f32[65536,128]{0,1:T(8,128)}) %all-gather.11.cloned.1.call-update) | async-done | bytes 33554448 | tf_op jit(solution)/shard_map/all_gather | solution.py:37
  1199.8 28.2 %copy.12 = f32[16,8,32,2048]{3,2,1,0:T(8,128)S(1)} copy(f32[16,8,32,2048]{3,1,2,0:T(8,128)} %bitcast.67) | data formatting | bytes 67108864
  1228.0 6.9 bitcast_reduce_fusion
  1234.9 1.0 copy-done.2
  1235.9 1.0 multiply_reduce_fusion.1
  1236.9 23.1 %psum.76 = f32[]{:T(128)} all-reduce(f32[]{:T(128)} %multiply_reduce_fusion.1), channel_id=1, replica_groups=mesh['dp'=32,'param'=16] {'param'}, use_global_device_ids=true, to_apply=%region_13.0 | all-reduce | flops 1 | bytes 8 | tf_op jit(solution)/shard_map/psum | solution.py:49
  1261.3 3.4 multiply_reduce_fusion
  1264.8 24.2 %psum.77 = f32[]{:T(128)} all-reduce(f32[]{:T(128)} %get-tuple-element.8), channel_id=1, replica_groups=mesh['dp'=32,'param'=16] {'param'}, use_global_device_ids=true, to_apply=%region_15.0 | all-reduce | flops 1 | bytes 8 | tf_op jit(solution)/shard_map/psum | solution.py:49
  1289.6 4.6 fusion.14
  1295.0 0.9 dynamic-slice_multiply_fusion
  1295.9 103.6 %all-reduce.12.cloned.1.call-done = f32[1024,36]{0,1:T(8,128)} async-done(((f32[1024,36]{0,1:T(8,128)}), f32[1024,36]{0,1:T(8,128)}) %all-reduce.12.cloned.1.call-update) | async-done | bytes 147472 | tf_op jit(solution)/shard_map/psum | solution.py:25
  1399.5 1.6 multiply_reduce_fusion.5
  1401.8 0.7 copy.9
  1402.5 75.8 %psum.79 = f32[]{:T(128)} all-reduce(f32[]{:T(128)S(6)} %div.38), channel_id=1, replica_groups=mesh['dp'=32,'param'=16] {'dp'}, use_global_device_ids=true, to_apply=%region_18.0 | all-reduce | flops 1 | bytes 8 | tf_op jit(solution)/shard_map/psum | solution.py:77
  (19 shorter events, 0.1 us)
Async XLA Ops:
  7.2 1.1 copy-start
  7.2 4.5 copy-start.3
  7.2 5.5 copy-start.7
  7.2 117.8 %copy-start.5 = (f32[1024,36]{0,1:T(8,128)S(1)}, f32[1024,36]{0,1:T(8,128)}, u32[]{:S(2)}) copy-start(f32[1024,36]{0,1:T(8,128)} %param.10) | copy-start | bytes 442372
  7.2 117.8 %copy-start.4 = (f32[1024,36]{0,1:T(8,128)S(1)}, f32[1024,36]{0,1:T(8,128)}, u32[]{:S(2)}) copy-start(f32[1024,36]{0,1:T(8,128)} %param.11) | copy-start | bytes 442372
  7.2 117.8 %copy-start.6 = (f32[1024]{0:T(1024)S(1)}, f32[1024]{0:T(1024)}, u32[]{:S(2)}) copy-start(f32[1024]{0:T(1024)} %param.12) | copy-start | bytes 12292
  7.2 117.8 %all-reduce.6.cloned.1.call-start = ((), (), s32[]{:S(2)}) async-start(), calls=%async_computation | async-start | bytes 327680 | tf_op jit(solution)/shard_map/psum | solution.py:25
  12.6 357.2 %all-gather.7.cloned.1.call-start = ((), (), s32[]{:S(2)}) async-start(), calls=%async_computation.4 | async-start | bytes 34603008 | tf_op jit(solution)/shard_map/all_gather | solution.py:37
  130.6 382.9 %all-reduce.8.cloned.1.call-start = ((), (), s32[]{:S(2)}) async-start(), calls=%async_computation.1 | async-start | bytes 327680 | tf_op jit(solution)/shard_map/psum | solution.py:25
  409.2 349.1 %all-gather.9.cloned.1.call-start = ((), (), s32[]{:S(2)}) async-start(), calls=%async_computation.5 | async-start | bytes 34603008 | tf_op jit(solution)/shard_map/all_gather | solution.py:37
  519.0 435.9 %all-reduce.10.cloned.1.call-start = ((), (), s32[]{:S(2)}) async-start(), calls=%async_computation.2 | async-start | bytes 327680 | tf_op jit(solution)/shard_map/psum | solution.py:25
  849.5 350.3 %all-gather.11.cloned.1.call-start = ((), (), s32[]{:S(2)}) async-start(), calls=%async_computation.6 | async-start | bytes 34603008 | tf_op jit(solution)/shard_map/all_gather | solution.py:37
  960.5 439.0 %all-reduce.12.cloned.1.call-start = ((), (), s32[]{:S(2)}) async-start(), calls=%async_computation.3 | async-start | bytes 327680 | tf_op jit(solution)/shard_map/psum | solution.py:25
  1234.9 1.0 copy-start.2
  1261.3 217.6 %copy-start.1 = (bf16[2048,128]{1,0:T(8,128)(2,1)S(1)}, bf16[2048,128]{1,0:T(8,128)(2,1)}, u32[]{:S(2)}) copy-start(bf16[2048,128]{1,0:T(8,128)(2,1)} %param.8) | copy-start | bytes 1572868
Sparse Core Ops, SparseCore 0:
  12.7 112.2 all-reduce.5
  130.7 239.1 all-gather.6
  409.4 104.0 all-reduce.7
  519.1 239.1 all-gather.8
  849.6 105.2 all-reduce.9
  960.6 239.1 all-gather.10
  1294.4 105.1 all-reduce.11
